TPU v7x, 32 devices: a whole 2x2x4 slice. The times are simulated.
32 devices in a mesh: seq: 8 (over z, x), head: 4 (over y, core).
Axes of the slice: x: 2, y: 2, z: 4, core: 2. Of those that a mesh axis runs over, the one named last changes fastest.
Arguments:
- queries: bfloat16 [4096, 4096], P('seq', 'head'), may hold values from -360 to 360, as said below
- key_rows: bfloat16 [4096, 1024], P('seq', 'head'), may hold values from -6 to 6
- value_rows: bfloat16 [4096, 1024], P('seq', 'head'), may hold values from -6 to 6
- doc_lengths: int32 [8], replicated, may hold values from 1 to 1536, 4096 in all
Outputs:
- attn_out: bfloat16 [4096, 4096], P(('seq', 'head'))
Inputs may be any that keep to these rules, and one draw needn't show every extreme that they name: `queries`: custom draw of bounded query entries. `doc_lengths`: the lengths sum to 4096; each is at most 1536.
All inputs are finite; a program needn't handle non-finite values.
Results may differ from a plain program's by a relative error of at most 0.0036.
Values may be sent and summed in bfloat16 or wider, within the bound.
A program may use at most 64 MiB of HBM per device.

v0:
```python
import jax
import jax.numpy as jnp
from jax import lax
from jax.sharding import PartitionSpec as P

H = 32
KVH = 8
HD = 128
SPAN = 4


scaling = 0.08838834764831845


def from_behind(x, axis, by):
    peers = lax.axis_size(axis)
    pairs = [(i, i + by) for i in range(peers) if 0 <= i + by < peers]
    return lax.ppermute(x, axis, pairs)


def doc_index(ends, positions):
    return jnp.sum((ends[None, :] <= positions[:, None]).astype(jnp.int32), axis=1)


def per_device(queries, key_rows, value_rows, doc_lengths):
    tokens_here = queries.shape[0]
    local_groups = key_rows.shape[1] // HD
    group = H // KVH
    key_window = key_rows
    value_window = value_rows
    for level in range(SPAN.bit_length() - 1):
        moved = from_behind((key_window, value_window), "seq", 1 << level)
        key_window = jnp.concatenate([moved[0], key_window], 0)
        value_window = jnp.concatenate([moved[1], value_window], 0)
    ends = jnp.cumsum(doc_lengths)
    first = lax.axis_index("seq") * tokens_here
    query_pos = first + jnp.arange(tokens_here, dtype=jnp.int32)
    key_pos = first - (SPAN - 1) * tokens_here + jnp.arange(SPAN * tokens_here, dtype=jnp.int32)
    allowed = (
        (key_pos[None, :] >= 0)
        & (doc_index(ends, key_pos)[None, :] == doc_index(ends, query_pos)[:, None])
        & (key_pos[None, :] <= query_pos[:, None])
    )
    outputs = []
    for kv_head in range(local_groups):
        key_head = key_window[:, kv_head * HD : (kv_head + 1) * HD]
        value_head = value_window[:, kv_head * HD : (kv_head + 1) * HD]
        for member in range(group):
            column = (kv_head * group + member) * HD
            query_head = queries[:, column : column + HD]
            scores = (
                lax.dot_general(
                    query_head,
                    key_head,
                    (((1,), (1,)), ((), ())),
                    preferred_element_type=jnp.float32,
                )
                * scaling
            )
            scores = jnp.where(allowed, scores, jnp.float32(-1e30))
            largest = jnp.max(scores, axis=1, keepdims=True)
            weights = jnp.where(allowed, jnp.exp(scores - largest), jnp.float32(0.0))
            total = jnp.sum(weights, axis=1, keepdims=True)
            mixed = jnp.dot(
                weights.astype(jnp.bfloat16), value_head, preferred_element_type=jnp.float32
            )
            outputs.append((mixed / total).astype(jnp.bfloat16))
    merged = jnp.concatenate(outputs, 1)
    return lax.all_to_all(merged, "head", split_axis=0, concat_axis=1, tiled=True)


def solution(mesh):
    in_specs = (P("seq", "head"), P("seq", "head"), P("seq", "head"), P())
    out_specs = P(("seq", "head"), None)
    return jax.shard_map(
        per_device, mesh=mesh, in_specs=in_specs, out_specs=out_specs, check_vma=False
    )
```

profile of v0, /device:TPU:16, one launch (start us, length us, event | category | flops | bytes accessed | tf_op | source)
XLA Modules:
  0.0 113.6 jit_solution(17404384899668671327)
XLA Ops:
  0.0 3.5 %collective-permute-start = (bf16[512,256]{1,0:T(8,128)(2,1)}, bf16[512,256]{1,0:T(8,128)(2,1)S(1)}, u32[]{:S(2)}, u32[]{:S(2)}) collective-permute-start(bf16[512,256]{1,0:T(8,128)(2,1)} %param.5), channel_id=1, source_target_pairs={{0,4},{4,8},{8,12},{12,16},{16,20},{20,24},{24,28},{1,5},{5,9},{9,... | collective-permute-start | bytes 786440 | tf_op jit(solution)/shard_map/ppermute | solution.py:18
  3.5 3.5 %collective-permute-start.2 = (bf16[512,256]{1,0:T(8,128)(2,1)}, bf16[512,256]{1,0:T(8,128)(2,1)S(1)}, u32[]{:S(2)}, u32[]{:S(2)}) collective-permute-start(bf16[512,256]{1,0:T(8,128)(2,1)} %param.6), channel_id=1, source_target_pairs={{0,4},{4,8},{8,12},{12,16},{16,20},{20,24},{24,28},{1,5},{5,9},{9,... | collective-permute-start | bytes 786440 | tf_op jit(solution)/shard_map/ppermute | solution.py:18
  7.0 5.3 %collective-permute-done = bf16[512,256]{1,0:T(8,128)(2,1)S(1)} collective-permute-done((bf16[512,256]{1,0:T(8,128)(2,1)}, bf16[512,256]{1,0:T(8,128)(2,1)S(1)}, u32[]{:S(2)}, u32[]{:S(2)}) %collective-permute-start) | collective-permute-done | bytes 262176 | tf_op jit(solution)/shard_map/ppermute | solution.py:18
  12.3 1.0 pad_maximum_fusion
  13.3 3.5 %collective-permute-start.1 = (bf16[1024,256]{1,0:T(8,128)(2,1)S(1)}, bf16[1024,256]{1,0:T(8,128)(2,1)S(1)}, u32[]{:S(2)}, u32[]{:S(2)}) collective-permute-start(bf16[1024,256]{1,0:T(8,128)(2,1)S(1)} %pad_maximum_fusion), channel_id=1, source_target_pairs={{0,8},{4,12},{8,16},{12,20},{16,24},{20,28},{1,9},{5,13},{9,17},{1... | collective-permute-start | bytes 1572872 | tf_op jit(solution)/shard_map/ppermute | solution.py:18
  16.8 0.8 reduce-window.8
  17.9 1.0 pad_maximum_fusion.1
  18.9 3.5 %collective-permute-start.3 = (bf16[1024,256]{1,0:T(8,128)(2,1)S(1)}, bf16[1024,256]{1,0:T(8,128)(2,1)S(1)}, u32[]{:S(2)}, u32[]{:S(2)}) collective-permute-start(bf16[1024,256]{1,0:T(8,128)(2,1)S(1)} %pad_maximum_fusion.1), channel_id=1, source_target_pairs={{0,8},{4,12},{8,16},{12,20},{16,24},{20,28},{1,9},{5,13},{9,17},{1... | collective-permute-start | bytes 1572872 | tf_op jit(solution)/shard_map/ppermute | solution.py:18
  22.4 7.6 %collective-permute-done.1 = bf16[1024,256]{1,0:T(8,128)(2,1)S(1)} collective-permute-done((bf16[1024,256]{1,0:T(8,128)(2,1)S(1)}, bf16[1024,256]{1,0:T(8,128)(2,1)S(1)}, u32[]{:S(2)}, u32[]{:S(2)}) %collective-permute-start.1) | collective-permute-done | bytes 524320 | tf_op jit(solution)/shard_map/ppermute | solution.py:18
  30.0 1.0 constant_dynamic-update-slice_fusion
  31.0 2.7 %fusion.130 = f32[2048,512]{1,0:T(8,128)} fusion(bf16[2048,256]{1,0:T(8,128)(2,1)S(1)} %constant_dynamic-update-slice_fusion, bf16[512,1024]{1,0:T(8,128)(2,1)S(1)} %copy-done.4), kind=kOutput, calls=%fused_computation.94 | convolution fusion | flops 268435456 | bytes 4849664 | tf_op jit(solution)/shard_map/dot_general | solution.py:52
  34.4 0.7 fusion.120
  35.1 0.7 fusion.118
  35.9 0.7 fusion.122
  36.6 0.7 fusion.134
  37.3 0.8 collective-permute-done.3
  38.1 1.3 %constant_dynamic-update-slice_fusion.5 = bf16[2048,256]{1,0:T(8,128)(2,1)} fusion(bf16[1024,256]{1,0:T(8,128)(2,1)S(1)} %collective-permute-done.3), kind=kLoop, calls=%fused_computation.114 | loop fusion | bytes 1048576
  39.4 0.7 constant_dynamic-update-slice_fusion.4
  40.1 0.7 constant_dynamic-update-slice_fusion.3
  40.9 4.0 %fusion.7 = (f32[512]{0:T(512)S(1)}, f32[512]{0:T(512)S(1)}, f32[2048,512]{1,0:T(8,128)}) fusion(s32[512]{0:T(512)S(1)} %iota_add_fusion.1, s32[2048]{0:T(1024)S(1)} %iota_add_fusion, s32[512]{0:T(512)S(1)} %convert_reduce_fusion.1, s32[2048]{0:T(1024)S(1)} %convert_reduce_fusion, pred[2048]{0:T(1024)(128)(4,1)S(1)} %broadcast_compare_fusion, ...), kind=kOutput, calls=%fused_computation.24 | convolution fusion | flops 278920192 | bytes 9070592 | tf_op jit(solution)/shard_map/dot_general | solution.py:52
  44.9 12.3 %fusion.22 = (f32[512]{0:T(512)S(1)}, f32[512]{0:T(512)S(1)}, f32[512]{0:T(512)S(1)}, f32[512]{0:T(512)S(1)}, f32[512]{0:T(512)S(1)}, /*index=5*/f32[512]{0:T(51...) fusion(f32[2048,512]{1,0:T(8,128)} %get-tuple-element.21, f32[512]{0:T(512)S(1)} %get-tuple-element.13, ...), kind=kOutput, calls=%fused_computation.39 | convolution fusion | flops 301985792 | bytes 34252800 | tf_op jit(solution)/shard_map/dot_general | solution.py:52
  57.2 5.8 %fusion.46 = bf16[512,1024]{0,1:T(8,128)(2,1)S(1)} fusion(f32[2048,512]{1,0:T(8,128)} %copy-done.2, f32[512]{0:T(512)S(1)} %get-tuple-element.14, bf16[2048,256]{1,0:T(8,128)(2,1)} %constant_dynamic-update-slice_fusion.3, f32[512]{0:T(512)S(1)} %get-tuple-element.12, s32[512]{0:T(512)S(1)} %iota_add_fusion.1, s32[512]{0:T(512)S(1)} %convert_reduce_fusion.1, ...), kind=kOutput, calls=%fused_computation.51 | convolution fusion | flops 278003712 | bytes 4876288 | tf_op jit(solution)/shard_map/dot_general | solution.py:64
  63.0 9.1 %fusion.20 = (f32[512]{0:T(512)S(1)}, f32[512]{0:T(512)S(1)}, f32[512]{0:T(512)S(1)}, f32[512]{0:T(512)S(1)}, f32[512]{0:T(512)S(1)}, /*index=5*/f32[512]{0:T(512)S(1)}) fusion(f32[2048,512]{1,0:T(8,128)S(1)} %fusion.118, f32[512]{0:T(512)S(1)} %get-tuple-element.11, s32[512]{0:T(512)S(1)} %iota_add_fusion.1, s32[2048]{0:T(1024)S(1)} %iota_add_fusion, ...), kind=kLoop, calls=%fused_computation.37 | loop fusion | flops 35648512 | bytes 25212928 | tf_op jit(solution)/shard_map/reduce_sum | solution.py:63
  72.0 3.2 %fusion.55 = bf16[512,1024]{0,1:T(8,128)(2,1)S(1)} fusion(bf16[512,1024]{0,1:T(8,128)(2,1)S(1)} %fusion.46, f32[2048,512]{1,0:T(8,128)S(1)} %copy-done.1, f32[512]{0:T(512)S(1)} %get-tuple-element.6, bf16[2048,256]{1,0:T(8,128)(2,1)} %constant_dynamic-update-slice_fusion.3, f32[512]{0:T(512)S(1)} %get-tuple-element.16, s32[512]{0:T(512)S(1)} %iota_add_fusion.1, ...), kind=kOutput, calls=%fused_computation.54 | convolution fusion | flops 278003712 | bytes 4876288 | tf_op jit(solution)/shard_map/dot_general | solution.py:64
  75.3 3.2 %fusion.64 = bf16[512,1024]{0,1:T(8,128)(2,1)S(1)} fusion(bf16[512,1024]{0,1:T(8,128)(2,1)S(1)} %fusion.55, f32[2048,512]{1,0:T(8,128)S(1)} %copy-done, f32[512]{0:T(512)S(1)} %get-tuple-element.7, bf16[2048,256]{1,0:T(8,128)(2,1)} %constant_dynamic-update-slice_fusion.3, f32[512]{0:T(512)S(1)} %get-tuple-element.17, s32[512]{0:T(512)S(1)} %iota_add_fusion.1, ...), kind=kOutput, calls=%fused_computation.57 | convolution fusion | flops 278003712 | bytes 4876288 | tf_op jit(solution)/shard_map/dot_general | solution.py:64
  78.5 3.2 %fusion.73 = bf16[512,1024]{0,1:T(8,128)(2,1)S(1)} fusion(bf16[512,1024]{0,1:T(8,128)(2,1)S(1)} %fusion.64, f32[2048,512]{1,0:T(8,128)S(1)} %fusion.128, f32[512]{0:T(512)S(1)} %get-tuple-element.8, bf16[2048,256]{1,0:T(8,128)(2,1)} %constant_dynamic-update-slice_fusion.3, f32[512]{0:T(512)S(1)} %get-tuple-element.18, s32[512]{0:T(512)S(1)} %iota_add_fusion.1, ...), kind=kOutput, calls=%fused_computation.60 | convolution fusion | flops 278003712 | bytes 4876288 | tf_op jit(solution)/shard_map/dot_general | solution.py:64
  81.8 3.2 %fusion.82 = bf16[512,1024]{0,1:T(8,128)(2,1)S(1)} fusion(bf16[512,1024]{0,1:T(8,128)(2,1)S(1)} %fusion.73, f32[2048,512]{1,0:T(8,128)S(1)} %fusion.122, f32[512]{0:T(512)S(1)} %get-tuple-element.9, bf16[2048,256]{1,0:T(8,128)(2,1)} %constant_dynamic-update-slice_fusion.3, f32[512]{0:T(512)S(1)} %get-tuple-element.19, s32[512]{0:T(512)S(1)} %iota_add_fusion.1, ...), kind=kOutput, calls=%fused_computation.63 | convolution fusion | flops 278003712 | bytes 4876288 | tf_op jit(solution)/shard_map/dot_general | solution.py:64
  85.0 3.2 %fusion.91 = bf16[512,1024]{0,1:T(8,128)(2,1)S(1)} fusion(bf16[512,1024]{0,1:T(8,128)(2,1)S(1)} %fusion.82, f32[2048,512]{1,0:T(8,128)S(1)} %fusion.120, f32[512]{0:T(512)S(1)} %get-tuple-element.10, bf16[2048,256]{1,0:T(8,128)(2,1)} %constant_dynamic-update-slice_fusion.3, f32[512]{0:T(512)S(1)} %get-tuple-element.20, s32[512]{0:T(512)S(1)} %iota_add_fusion.1, ...), kind=kOutput, calls=%fused_computation.66 | convolution fusion | flops 278003712 | bytes 4876288 | tf_op jit(solution)/shard_map/dot_general | solution.py:64
  88.3 3.6 %fusion.100 = bf16[512,1024]{0,1:T(8,128)(2,1)S(1)} fusion(bf16[512,1024]{0,1:T(8,128)(2,1)S(1)} %fusion.91, f32[2048,512]{1,0:T(8,128)S(1)} %fusion.118, f32[512]{0:T(512)S(1)} %get-tuple-element.11, bf16[2048,256]{1,0:T(8,128)(2,1)} %constant_dynamic-update-slice_fusion.3, f32[512]{0:T(512)S(1)} %get-tuple-element.15, s32[512]{0:T(512)S(1)} %iota_add_fusion.1, ...), kind=kOutput, calls=%fused_computation.69 | convolution fusion | flops 278003712 | bytes 4876288 | tf_op jit(solution)/shard_map/dot_general | solution.py:64
  91.9 3.2 %fusion.109 = bf16[512,1024]{0,1:T(8,128)(2,1)S(1)} fusion(bf16[512,1024]{0,1:T(8,128)(2,1)S(1)} %fusion.100, f32[2048,512]{1,0:T(8,128)S(1)} %copy-done.5, f32[512]{0:T(512)S(1)} %get-tuple-element.13, bf16[2048,256]{1,0:T(8,128)(2,1)} %constant_dynamic-update-slice_fusion.3, f32[512]{0:T(512)S(1)} %get-tuple-element.5, s32[512]{0:T(512)S(1)} %iota_add_fusion.1, ...), kind=kOutput, calls=%fused_computation.72 | convolution fusion | flops 278003712 | bytes 4876288 | tf_op jit(solution)/shard_map/dot_general | solution.py:64
  95.3 17.0 %all_to_all.19 = bf16[4,128,1024]{1,2,0:T(8,128)(2,1)S(1)} all-to-all(bf16[4,128,1024]{1,2,0:T(8,128)(2,1)S(1)} %copy_bitcast_fusion), channel_id=1, replica_groups=mesh['seq'=8,'head'=4] {'head'}, dimensions={0} | all-to-all | bytes 2097152 | tf_op jit(solution)/shard_map/all_to_all | solution.py:69
  112.3 1.3 %copy.9 = bf16[128,4096]{1,0:T(8,128)(2,1)} copy(bf16[128,4096]{0,1:T(8,128)(2,1)S(1)} %bitcast.146) | data formatting | bytes 2097152 | tf_op jit(solution)/shard_map/all_to_all | solution.py:69
  (22 shorter events, 1.3 us)
Async XLA Ops:
  0.0 31.0 %copy-start.4 = (bf16[512,1024]{1,0:T(8,128)(2,1)S(1)}, bf16[512,1024]{1,0:T(8,128)(2,1)}, u32[]{:S(2)}) copy-start(bf16[512,1024]{1,0:T(8,128)(2,1)} %param.4) | copy-start | bytes 3145732
  0.0 12.3 %collective-permute-start = (bf16[512,256]{1,0:T(8,128)(2,1)}, bf16[512,256]{1,0:T(8,128)(2,1)S(1)}, u32[]{:S(2)}, u32[]{:S(2)}) collective-permute-start(bf16[512,256]{1,0:T(8,128)(2,1)} %param.5), channel_id=1, source_target_pairs={{0,4},{4,8},{8,12},{12,16},{16,20},{20,24},{24,28},{1,5},{5,9},{9,... | collective-permute-start | bytes 786440 | tf_op jit(solution)/shard_map/ppermute | solution.py:18
  3.5 14.4 %collective-permute-start.2 = (bf16[512,256]{1,0:T(8,128)(2,1)}, bf16[512,256]{1,0:T(8,128)(2,1)S(1)}, u32[]{:S(2)}, u32[]{:S(2)}) collective-permute-start(bf16[512,256]{1,0:T(8,128)(2,1)} %param.6), channel_id=1, source_target_pairs={{0,4},{4,8},{8,12},{12,16},{16,20},{20,24},{24,28},{1,5},{5,9},{9,... | collective-permute-start | bytes 786440 | tf_op jit(solution)/shard_map/ppermute | solution.py:18
  13.3 16.7 %collective-permute-start.1 = (bf16[1024,256]{1,0:T(8,128)(2,1)S(1)}, bf16[1024,256]{1,0:T(8,128)(2,1)S(1)}, u32[]{:S(2)}, u32[]{:S(2)}) collective-permute-start(bf16[1024,256]{1,0:T(8,128)(2,1)S(1)} %pad_maximum_fusion), channel_id=1, source_target_pairs={{0,8},{4,12},{8,16},{12,20},{16,24},{20,28},{1,9},{5,13},{9,17},{1... | collective-permute-start | bytes 1572872 | tf_op jit(solution)/shard_map/ppermute | solution.py:18
  18.9 19.2 %collective-permute-start.3 = (bf16[1024,256]{1,0:T(8,128)(2,1)S(1)}, bf16[1024,256]{1,0:T(8,128)(2,1)S(1)}, u32[]{:S(2)}, u32[]{:S(2)}) collective-permute-start(bf16[1024,256]{1,0:T(8,128)(2,1)S(1)} %pad_maximum_fusion.1), channel_id=1, source_target_pairs={{0,8},{4,12},{8,16},{12,20},{16,24},{20,28},{1,9},{5,13},{9,17},{1... | collective-permute-start | bytes 1572872 | tf_op jit(solution)/shard_map/ppermute | solution.py:18
  36.6 3.6 %copy-start.3 = (bf16[512,256]{1,0:T(8,128)(2,1)S(1)}, bf16[512,256]{1,0:T(8,128)(2,1)}, u32[]{:S(2)}) copy-start(bf16[512,256]{1,0:T(8,128)(2,1)} %param.6) | copy-start | bytes 786436
  37.3 7.6 %copy-start.2 = (f32[2048,512]{1,0:T(8,128)}, f32[2048,512]{1,0:T(8,128)S(1)}, u32[]{:S(2)}) copy-start(f32[2048,512]{1,0:T(8,128)S(1)} %fusion.134) | copy-start | bytes 12582916
  57.1 5.8 %copy-start = (f32[2048,512]{1,0:T(8,128)S(1)}, f32[2048,512]{1,0:T(8,128)}, u32[]{:S(2)}) copy-start(f32[2048,512]{1,0:T(8,128)} %fusion.130) | copy-start | bytes 12582916
  57.1 5.8 %copy-start.1 = (f32[2048,512]{1,0:T(8,128)S(1)}, f32[2048,512]{1,0:T(8,128)}, u32[]{:S(2)}) copy-start(f32[2048,512]{1,0:T(8,128)} %get-tuple-element.22) | copy-start | bytes 12582916
  88.3 3.6 %copy-start.5 = (f32[2048,512]{1,0:T(8,128)S(1)}, f32[2048,512]{1,0:T(8,128)}, u32[]{:S(2)}) copy-start(f32[2048,512]{1,0:T(8,128)} %get-tuple-element.21) | copy-start | bytes 12582916
where the time goes:
time: 115 us; the launch traced here: 114 us
  matrix products  51.3 us (45%)
  blocking collectives  17 us (15%)
  starting transfers between devices  13.9 us (12%)
  waiting for transfers between devices  13.8 us (12%)
  other arithmetic  12.1 us (11%)
  local copies, waits for them, and re-layouts  5.29 us (5%)
    dot_general x8, matrix products, per_device(): jnp.dot(weights.astype(jnp.bfloat16), value_head, preferred_element_type=...  28.8 us
    dot_general x8, matrix products, per_device(): lax.dot_general(query_head, key_head, (((1,), (1,)), ((), ())), preferred...  22.5 us
    all_to_all x1, blocking collectives, per_device(): lax.all_to_all(merged, 'head', split_axis=0, concat_axis=1, tiled=True)  17 us
    ppermute x4, starting transfers between devices, from_behind(): return lax.ppermute(x, axis, pairs)  13.9 us
    ppermute x4, waiting for transfers between devices, from_behind(): return lax.ppermute(x, axis, pairs)  13.8 us
    reduce_sum x1, other arithmetic, per_device(): total = jnp.sum(weights, axis=1, keepdims=True)  9.06 us
  transfers between devices with their start and end apart: 4, of which 4 were waited for; matrix products, arithmetic and copies ran while one was open for 9% of the time, Pallas kernels for 0%

commit v1 on v0

v1 whole, which is shorter than its diff:
```python
import functools
import math

import jax
import jax.numpy as jnp
from jax import lax
from jax.experimental import pallas as pl
from jax.experimental.pallas import tpu as pltpu
from jax.sharding import PartitionSpec as P

H = 32
KVH = 8
HD = 128
SPAN = 4
FAR = -1e30
GROUP = H // KVH
EXP2_SCALE = 0.08838834764831845 * math.log2(math.e)
MESH = pl.DeviceIdType.MESH


def kernel(
    n_seq, n_head, doc_ref, q_hbm, k_hbm, v_hbm, out_ref,
    qbuf, kbuf, vbuf, qdoc, kdoc, obuf,
    load_sem, send_sem, recv_sem, out_send, out_recv, own_sem,
):
    b = lax.axis_index("seq")
    h = lax.axis_index("head")
    tokens = q_hbm.shape[0]
    groups = k_hbm.shape[1] // HD
    tile = tokens // n_head
    width = GROUP * HD
    window = SPAN * tokens
    reach = (SPAN - 1) * tokens
    even = b % 2 == 0
    odd = b % 2 == 1
    bufs = (kbuf, vbuf)

    loads = []
    for g in range(groups):
        for a, source in enumerate((k_hbm, v_hbm)):
            loads.append(pltpu.make_async_copy(
                source.at[:, pl.ds(g * HD, HD)],
                bufs[a].at[g, pl.ds(reach, tokens), :],
                load_sem.at[g, a],
            ))
    for load in loads:
        load.start()
    q_load = pltpu.make_async_copy(q_hbm, qbuf, load_sem.at[groups, 0])
    q_load.start()

    barrier = pltpu.get_barrier_semaphore()
    partner = b + 1 - 2 * (b % 2)
    pl.semaphore_signal(barrier, inc=1, device_id={"seq": partner, "head": h}, device_id_type=MESH)
    for off in range(1, n_head):
        pl.semaphore_signal(
            barrier, inc=1, device_id={"seq": b, "head": (h + off) % n_head}, device_id_type=MESH
        )

    @pl.when(b + 2 < n_seq)
    def _():
        pl.semaphore_signal(barrier, inc=1, device_id={"seq": b + 2, "head": h}, device_id_type=MESH)

    @pl.when(b >= 2)
    def _():
        pl.semaphore_signal(barrier, inc=1, device_id={"seq": b - 2, "head": h}, device_id_type=MESH)

    beyond = jnp.where(b + 2 < n_seq, 1, 0) + jnp.where(b >= 2, 1, 0)
    pl.semaphore_wait(barrier, n_head + beyond)

    def hop(kind, g, a, source, target, slot):
        return pltpu.make_async_remote_copy(
            src_ref=bufs[a].at[g, pl.ds(source * tokens, tokens), :],
            dst_ref=bufs[a].at[g, pl.ds(slot * tokens, tokens), :],
            send_sem=send_sem.at[kind, g, a],
            recv_sem=recv_sem.at[slot, g, a],
            device_id={"seq": target, "head": h},
            device_id_type=MESH,
        )

    own = SPAN - 1

    def send_own(g, a):
        @pl.when(even)
        def _():
            hop(0, g, a, own, b + 1, 2).start()

        @pl.when(b + 2 < n_seq)
        def _():
            hop(1, g, a, own, b + 2, 1).start()

    def relay_odd(g, a):
        @pl.when(odd & (b >= 2))
        def _():
            hop(1, g, a, own, b - 2, 1).wait_recv()
            hop(2, g, a, 1, b - 1, 2).start()

    def relay_even(g, a):
        @pl.when(even & (b >= 2))
        def _():
            hop(1, g, a, own, b - 2, 1).wait_recv()
            hop(2, g, a, 1, b + 1, 0).start()
            hop(2, g, a, own, b + 1, 2).wait_recv()

        @pl.when(even & (b >= 2) & (b + 2 < n_seq))
        def _():
            hop(3, g, a, 2, b + 2, 0).start()

    def arrive(g, a):
        @pl.when(odd)
        def _():
            hop(0, g, a, own, b - 1, 2).wait_recv()

        @pl.when(odd & (b >= 3))
        def _():
            hop(0, g, a, own, b - 1, 0).wait_recv()

        @pl.when(even & (b >= 4))
        def _():
            hop(0, g, a, own, b - 2, 0).wait_recv()

    def sent(g, a):
        @pl.when(even)
        def _():
            hop(0, g, a, own, b + 1, 2).wait_send()

        @pl.when(b + 2 < n_seq)
        def _():
            hop(1, g, a, own, b + 2, 1).wait_send()

        @pl.when(b >= 2)
        def _():
            hop(2, g, a, 1, partner, 0).wait_send()

        @pl.when(even & (b >= 2) & (b + 2 < n_seq))
        def _():
            hop(3, g, a, 2, b + 2, 0).wait_send()

    for a in range(2):
        loads[a].wait()
        send_own(0, a)
    for g in range(1, groups):
        for a in range(2):
            loads[g * 2 + a].wait()

            @pl.when(odd)
            def _():
                send_own(g, a)

    lane = lax.broadcasted_iota(jnp.int32, (1, HD), 1)
    low = jnp.full((1, HD), 1 << 30, jnp.int32)
    high = jnp.full((1, HD), 0, jnp.int32)
    end = jnp.int32(0)
    for d in range(doc_ref.shape[0]):
        start = end
        end = end + doc_ref[d]
        low = jnp.where(lane == d, start, low)
        high = jnp.where(lane == d, end, high)
    first = b * tokens

    def key_docs(i, _):
        rows = i * tile
        pos = first - reach + rows + lax.broadcasted_iota(jnp.int32, (tile, HD), 0)
        same = (pos >= low) & (pos < high)
        kdoc[pl.ds(rows, tile), :] = jnp.where(same, 0.0, FAR).astype(jnp.bfloat16)
        return 0

    lax.fori_loop(0, window // tile, key_docs, 0)

    def query_docs(i, _):
        rows = i * tile
        pos = first + rows + lax.broadcasted_iota(jnp.int32, (tile, HD), 0)
        same = (pos >= low) & (pos < high)
        qdoc[pl.ds(rows, tile), :] = jnp.where(same, 1.0, 0.0).astype(jnp.bfloat16)
        return 0

    lax.fori_loop(0, n_head, query_docs, 0)

    for slot in range(SPAN - 1):
        @pl.when(b < SPAN - 1 - slot)
        def _():
            for g in range(groups):
                for buf in bufs:
                    buf[g, slot * tokens:(slot + 1) * tokens, :] = jnp.zeros((tokens, HD), jnp.bfloat16)

    q_load.wait()
    for g in range(groups):
        for a in range(2):
            relay_odd(g, a)
    for a in range(2):
        relay_even(0, a)
    for g in range(1, groups):
        for a in range(2):
            @pl.when(even)
            def _():
                send_own(g, a)

    span = reach + tile
    ones = jnp.ones((span, HD), jnp.bfloat16)

    def deliver(g, off, t):
        return pltpu.make_async_remote_copy(
            src_ref=obuf.at[g, t],
            dst_ref=out_ref.at[:, pl.ds(pl.multiple_of((h * groups + g) * width, width), width)],
            send_sem=out_send.at[g, off - 1],
            recv_sem=out_recv.at[g, off - 1],
            device_id={"seq": b, "head": t},
            device_id_type=MESH,
        )

    def receive(g, off):
        source = (h + n_head - off) % n_head
        return pltpu.make_async_remote_copy(
            src_ref=obuf.at[g, 0],
            dst_ref=out_ref.at[:, pl.ds(pl.multiple_of((source * groups + g) * width, width), width)],
            send_sem=out_send.at[g, off - 1],
            recv_sem=out_recv.at[g, off - 1],
            device_id={"seq": b, "head": source},
            device_id_type=MESH,
        )

    def keep(g):
        return pltpu.make_async_copy(
            obuf.at[g, h],
            out_ref.at[:, pl.ds(pl.multiple_of((h * groups + g) * width, width), width)],
            own_sem.at[g],
        )

    def attend(g, t):
        rows = pl.ds(pl.multiple_of(t * tile, tile), tile)
        keys = pl.ds(pl.multiple_of(t * tile, tile), span)
        key_ext = jnp.concatenate([kbuf[g, keys, :], kdoc[keys, :]], 1)
        value_ext = jnp.concatenate([vbuf[g, keys, :], ones], 1)
        marks = qdoc[rows, :]
        below = lax.broadcasted_iota(jnp.int32, (tile, tile), 1) <= lax.broadcasted_iota(
            jnp.int32, (tile, tile), 0
        )
        pair = 2
        for part in range(GROUP // pair):
            query = jnp.concatenate([
                jnp.concatenate(
                    [qbuf[rows, (g * GROUP + part * pair + m) * HD:(g * GROUP + part * pair + m + 1) * HD], marks], 1
                )
                for m in range(pair)
            ], 0)
            scores = lax.dot_general(
                query, key_ext, (((1,), (1,)), ((), ())), preferred_element_type=jnp.float32
            )
            edge = jnp.where(jnp.concatenate([below] * pair, 0), scores[:, reach:], FAR)
            scores = jnp.concatenate([scores[:, :reach], edge], 1)
            largest = jnp.max(scores, axis=1, keepdims=True)
            weights = jnp.exp2((scores - largest) * EXP2_SCALE).astype(jnp.bfloat16)
            mixed = jnp.dot(weights, value_ext, preferred_element_type=jnp.float32)
            result = (mixed[:, :HD] / mixed[:, HD:]).astype(jnp.bfloat16)
            for m in range(pair):
                column = (part * pair + m) * HD
                obuf[g, t, :, column:column + HD] = result[m * tile:(m + 1) * tile]

    for g in range(groups):
        for a in range(2):
            arrive(g, a)

        def step(i, _):
            off = n_head - 1 - i
            t = (h + off) % n_head
            attend(g, t)
            if g + 1 < groups:
                @pl.when(i == 1)
                def _():
                    for a in range(2):
                        relay_even(g + 1, a)

            @pl.when(i < n_head - 1)
            def _():
                deliver(g, off, t).start()

            @pl.when(i == n_head - 1)
            def _():
                keep(g).start()
            return 0

        lax.fori_loop(0, n_head, step, 0)

    for g in range(groups):
        for a in range(2):
            sent(g, a)
    for g in range(groups):
        keep(g).wait()
        for off in range(1, n_head):
            deliver(g, off, (h + off) % n_head).wait_send()
            receive(g, off).wait_recv()


def per_device(n_seq, n_head, queries, key_rows, value_rows, doc_lengths):
    tokens = queries.shape[0]
    groups = key_rows.shape[1] // HD
    tile = tokens // n_head
    window = SPAN * tokens
    flops = 4 * tokens * (GROUP * groups) * window * HD
    return pl.pallas_call(
        functools.partial(kernel, n_seq, n_head),
        out_shape=jax.ShapeDtypeStruct((tile, H * HD), jnp.bfloat16),
        in_specs=[pl.BlockSpec(memory_space=pltpu.SMEM)]
        + [pl.BlockSpec(memory_space=pl.ANY)] * 3,
        out_specs=pl.BlockSpec(memory_space=pl.ANY),
        scratch_shapes=[
            pltpu.VMEM((tokens, GROUP * groups * HD), jnp.bfloat16),
            pltpu.VMEM((groups, window, HD), jnp.bfloat16),
            pltpu.VMEM((groups, window, HD), jnp.bfloat16),
            pltpu.VMEM((tokens, HD), jnp.bfloat16),
            pltpu.VMEM((window, HD), jnp.bfloat16),
            pltpu.VMEM((groups, n_head, tile, GROUP * HD), jnp.bfloat16),
            pltpu.SemaphoreType.DMA((groups + 1, 2)),
            pltpu.SemaphoreType.DMA((4, groups, 2)),
            pltpu.SemaphoreType.DMA((SPAN - 1, groups, 2)),
            pltpu.SemaphoreType.DMA((groups, n_head - 1)),
            pltpu.SemaphoreType.DMA((groups, n_head - 1)),
            pltpu.SemaphoreType.DMA((groups,)),
        ],
        compiler_params=pltpu.CompilerParams(
            collective_id=0, has_side_effects=True, vmem_limit_bytes=60 << 20
        ),
        cost_estimate=pl.CostEstimate(flops=flops, bytes_accessed=4 << 20, transcendentals=0),
    )(doc_lengths, queries, key_rows, value_rows)


def solution(mesh):
    body = functools.partial(per_device, mesh.shape["seq"], mesh.shape["head"])
    in_specs = (P("seq", "head"), P("seq", "head"), P("seq", "head"), P())
    out_specs = P(("seq", "head"), None)
    return jax.shard_map(body, mesh=mesh, in_specs=in_specs, out_specs=out_specs, check_vma=False)
```

time: 115 us -> 42.5 us (0.37); the launches traced: 114 us -> 42.4 us
  matrix products: 51.3 us -> 0 us
  Pallas kernels: 0 us -> 40.1 us
  blocking collectives: 17 us -> 0 us
  starting transfers between devices: 13.9 us -> 0 us
  waiting for transfers between devices: 13.8 us -> 0 us
  other arithmetic: 12.1 us -> 0 us
  local copies, waits for them, and re-layouts: 5.29 us -> 2.29 us
    dot_general x16 -> x0, matrix products: 51.3 us -> none  [the longest x8 28.8 us: per_device(): jnp.dot(weights.astype(jnp.bfloat16), value_head, preferred_element_type=...]
    pallas_call x0 -> x1, Pallas kernels: none -> 40.1 us  [per_device(): pl.pallas_call(functools.partial(kernel, n_seq, n_head), out_shape=jax.Sh...]
    all_to_all x1 -> x0, blocking collectives: 17 us -> none  [per_device(): lax.all_to_all(merged, 'head', split_axis=0, concat_axis=1, tiled=True)]
    ppermute x4 -> x0, starting transfers between devices: 13.9 us -> none  [from_behind(): return lax.ppermute(x, axis, pairs)]
    ppermute x4 -> x0, waiting for transfers between devices: 13.8 us -> none  [from_behind(): return lax.ppermute(x, axis, pairs)]
    reduce_sum x3 -> x0, other arithmetic: 9.23 us -> none  [the longest x1 9.06 us: per_device(): total = jnp.sum(weights, axis=1, keepdims=True)]
    concatenate x2 -> x0, other arithmetic: 1.97 us -> none  [the longest x1 0.98 us: per_device(): key_window = jnp.concatenate([moved[0], key_window], 0)]
    concatenate x2 -> x0, local copies, waits for them, and re-layouts: 1.69 us -> none  [the longest x1 0.97 us: per_device(): key_window = jnp.concatenate([moved[0], key_window], 0)]
  transfers between devices with their start and end apart: 4 -> 0, of which waited for: 4 -> 0; matrix products, arithmetic and copies ran while one was open for 9% -> 0% of each run, Pallas kernels for 0% -> 0%
where the time goes in v1:
time: 42.5 us; the launch traced here: 42.4 us
  Pallas kernels  40.1 us (94%)
  local copies, waits for them, and re-layouts  2.29 us (5%)
    pallas_call x1, Pallas kernels, per_device(): pl.pallas_call(functools.partial(kernel, n_seq, n_head), out_shape=jax.Sh...  40.1 us
    unnamed x1, local copies, waits for them, and re-layouts  2.29 us

profile of v1, /device:TPU:16, one launch (start us, length us, event | category | flops | bytes accessed | tf_op | source)
XLA Modules:
  0.0 42.4 jit_solution(12811005880923417806)
XLA Ops:
  0.0 40.1 %shard_map.46 = bf16[128,4096]{1,0:T(8,128)(2,1)} custom-call(s32[8]{0:T(128)} %doc_ref.1, bf16[512,1024]{1,0:T(8,128)(2,1)} %q_hbm.1, bf16[512,256]{1,0:T(8,128)(2,1)} %k_hbm.1, bf16[512,256]{1,0:T(8,128)(2,1)} %v_hbm.1), custom_call_target="tpu_custom_call" | custom-call | flops 4294967296 | bytes 4194304 | tf_op jit(solution)/shard_map/pallas_call | solution.py:299
  40.1 2.3 %copy.6 = bf16[128,4096]{1,0:T(8,128)(2,1)} copy(bf16[128,4096]{1,0:T(8,128)(2,1)} %shard_map.46) | data formatting | bytes 2097152

commit v2 on v1

v2 whole, which is shorter than its diff:
```python
import functools
import math

import jax
import jax.numpy as jnp
from jax import lax
from jax.experimental import pallas as pl
from jax.experimental.pallas import tpu as pltpu
from jax.sharding import PartitionSpec as P

H = 32
KVH = 8
HD = 128
SPAN = 4
FAR = -1e30
PAIR = 2
GROUP = H // KVH
EXP2_SCALE = 0.08838834764831845 * math.log2(math.e)
MESH = pl.DeviceIdType.MESH


def kernel(
    n_seq, n_head, doc_ref, q_hbm, k_hbm, v_hbm, out_ref,
    qbuf, kbuf, vbuf, qdoc, kdoc, obuf, peak, total,
    load_sem, send_sem, recv_sem, out_send, out_recv, own_sem,
):
    b = lax.axis_index("seq")
    h = lax.axis_index("head")
    tokens = q_hbm.shape[0]
    groups = k_hbm.shape[1] // HD
    tile = tokens // n_head
    width = GROUP * HD
    window = SPAN * tokens
    reach = (SPAN - 1) * tokens
    even = b % 2 == 0
    odd = b % 2 == 1
    bufs = (kbuf, vbuf)

    loads = []
    for g in range(groups):
        for a, source in enumerate((k_hbm, v_hbm)):
            loads.append(pltpu.make_async_copy(
                source.at[:, pl.ds(g * HD, HD)],
                bufs[a].at[g, pl.ds(reach, tokens), :],
                load_sem.at[g, a],
            ))
    for load in loads:
        load.start()
    q_load = pltpu.make_async_copy(q_hbm, qbuf, load_sem.at[groups, 0])
    q_load.start()

    barrier = pltpu.get_barrier_semaphore()
    partner = b + 1 - 2 * (b % 2)
    outer = b - 1 + 2 * (b % 2)
    has_next = b + 2 < n_seq
    has_last = b >= 2
    has_outer = (outer >= 0) & (outer < n_seq)

    def greet(seq, head):
        pl.semaphore_signal(
            barrier, inc=1, device_id={"seq": seq, "head": head}, device_id_type=MESH
        )

    greet(partner, h)
    for off in range(1, n_head):
        greet(b, (h + off) % n_head)
    for condition, seq in ((has_next, b + 2), (has_last, b - 2), (has_outer, outer)):
        @pl.when(condition)
        def _():
            greet(seq, h)

    beyond = sum(jnp.where(c, 1, 0) for c in (has_next, has_last, has_outer))
    pl.semaphore_wait(barrier, n_head + beyond)

    own = SPAN - 1
    cut = tokens // 48 * 16

    def hop(kind, g, a, source, target, slot, piece=None):
        start, size = {None: (0, tokens), 0: (0, cut), 1: (cut, tokens - cut)}[piece]
        landing = slot if piece != 1 else own
        return pltpu.make_async_remote_copy(
            src_ref=bufs[a].at[g, pl.ds(source * tokens + start, size), :],
            dst_ref=bufs[a].at[g, pl.ds(slot * tokens + start, size), :],
            send_sem=send_sem.at[kind, g, a],
            recv_sem=recv_sem.at[landing, g, a],
            device_id={"seq": target, "head": h},
            device_id_type=MESH,
        )

    def own_near(g, a):
        return hop(0, g, a, own, b + 1, 2)

    def own_far(g, a):
        return hop(1, g, a, own, b + 2, 1)

    def even_one(g, a):
        return hop(2, g, a, 1, b + 1, 0, 1)

    def even_two(g, a):
        return hop(3, g, a, 2, b + 2, 0, 1)

    def odd_back(g, a):
        return hop(2, g, a, 1, b - 1, 2)

    def odd_one(g, a):
        return hop(3, g, a, 1, b + 1, 0, 0)

    def odd_two(g, a):
        return hop(4, g, a, 2, b + 2, 0, 0)

    sends = (
        (even, own_near),
        (has_next, own_far),
        (even & has_last, even_one),
        (even & has_last & has_next, even_two),
        (odd & has_last, odd_back),
        (odd & has_last & has_outer, odd_one),
        (odd & has_next, odd_two),
    )

    def send_own(g, a):
        for condition, copy in sends[:2]:
            @pl.when(condition)
            def _():
                copy(g, a).start()

    def relay_one(parity, g, a):
        if parity == 0:
            @pl.when(even & has_last)
            def _():
                hop(1, g, a, own, b - 2, 1).wait_recv()
                even_one(g, a).start()
        else:
            @pl.when(odd & has_last)
            def _():
                hop(1, g, a, own, b - 2, 1).wait_recv()
                odd_back(g, a).start()

            @pl.when(odd & has_last & has_outer)
            def _():
                odd_one(g, a).start()

    def relay_two(parity, g, a):
        if parity == 0:
            @pl.when(even & has_last)
            def _():
                hop(2, g, a, own, b + 1, 2).wait_recv()

            @pl.when(even & has_last & has_next)
            def _():
                even_two(g, a).start()
        else:
            @pl.when(odd)
            def _():
                hop(0, g, a, own, b - 1, 2).wait_recv()

            @pl.when(odd & has_next)
            def _():
                odd_two(g, a).start()

    def arrive(g, a):
        @pl.when(b >= SPAN - 1)
        def _():
            hop(2, g, a, 1, b - 1, 0, 0).wait_recv()
            hop(2, g, a, 1, b - 1, 0, 1).wait_recv()

    def sent(g, a):
        for condition, copy in sends:
            @pl.when(condition)
            def _():
                copy(g, a).wait_send()

    for g in range(groups):
        for a in range(2):
            loads[g * 2 + a].wait()
            send_own(g, a)

    lane = lax.broadcasted_iota(jnp.int32, (1, HD), 1)
    low = jnp.full((1, HD), 1 << 30, jnp.int32)
    high = jnp.full((1, HD), 0, jnp.int32)
    end = jnp.int32(0)
    for d in range(doc_ref.shape[0]):
        start = end
        end = end + doc_ref[d]
        low = jnp.where(lane == d, start, low)
        high = jnp.where(lane == d, end, high)
    first = b * tokens

    def key_docs(i, _):
        rows = i * tile
        pos = first - reach + rows + lax.broadcasted_iota(jnp.int32, (tile, HD), 0)
        same = (pos >= low) & (pos < high)
        kdoc[pl.ds(rows, tile), :] = jnp.where(same, 0.0, FAR).astype(jnp.bfloat16)
        return 0

    lax.fori_loop(0, window // tile, key_docs, 0)

    def query_docs(i, _):
        rows = i * tile
        pos = first + rows + lax.broadcasted_iota(jnp.int32, (tile, HD), 0)
        same = (pos >= low) & (pos < high)
        qdoc[pl.ds(rows, tile), :] = jnp.where(same, 1.0, 0.0).astype(jnp.bfloat16)
        return 0

    lax.fori_loop(0, n_head, query_docs, 0)

    for slot in range(SPAN - 1):
        @pl.when(b < SPAN - 1 - slot)
        def _():
            for g in range(groups):
                for buf in bufs:
                    buf[g, slot * tokens:(slot + 1) * tokens, :] = jnp.zeros((tokens, HD), jnp.bfloat16)

    q_load.wait()
    for a in range(2):
        relay_one(0, 0, a)
        relay_one(1, 0, a)
        relay_two(1, 0, a)
    for a in range(2):
        relay_two(0, 0, a)

    near = tokens * (SPAN - 2) + tile
    far = tokens

    def deliver(g, off, t):
        return pltpu.make_async_remote_copy(
            src_ref=obuf.at[g, t],
            dst_ref=out_ref.at[:, pl.ds(pl.multiple_of((h * groups + g) * width, width), width)],
            send_sem=out_send.at[g, off - 1],
            recv_sem=out_recv.at[g, off - 1],
            device_id={"seq": b, "head": t},
            device_id_type=MESH,
        )

    def receive(g, off):
        source = (h + n_head - off) % n_head
        return pltpu.make_async_remote_copy(
            src_ref=obuf.at[g, 0],
            dst_ref=out_ref.at[:, pl.ds(pl.multiple_of((source * groups + g) * width, width), width)],
            send_sem=out_send.at[g, off - 1],
            recv_sem=out_recv.at[g, off - 1],
            device_id={"seq": b, "head": source},
            device_id_type=MESH,
        )

    def keep(g):
        return pltpu.make_async_copy(
            obuf.at[g, h],
            out_ref.at[:, pl.ds(pl.multiple_of((h * groups + g) * width, width), width)],
            own_sem.at[g],
        )

    below = lax.broadcasted_iota(jnp.int32, (tile, tile), 1) <= lax.broadcasted_iota(
        jnp.int32, (tile, tile), 0
    )
    parts = GROUP // PAIR
    block = PAIR * tile

    def queries(g, t, part):
        rows = pl.ds(pl.multiple_of(t * tile, tile), tile)
        marks = qdoc[rows, :]
        return jnp.concatenate([
            jnp.concatenate([qbuf[rows, column:column + HD], marks], 1)
            for column in ((g * GROUP + part * PAIR + m) * HD for m in range(PAIR))
        ], 0)

    def window_of(g, start, size):
        keys = pl.ds(pl.multiple_of(start, tile), size)
        key_ext = jnp.concatenate([kbuf[g, keys, :], kdoc[keys, :]], 1)
        value_ext = jnp.concatenate([vbuf[g, keys, :], jnp.ones((size, HD), jnp.bfloat16)], 1)
        return key_ext, value_ext

    def attend_near(g, t):
        key_ext, value_ext = window_of(g, t * tile + far, near)
        for part in range(parts):
            scores = lax.dot_general(
                queries(g, t, part), key_ext, (((1,), (1,)), ((), ())),
                preferred_element_type=jnp.float32,
            )
            edge = jnp.where(jnp.concatenate([below] * PAIR, 0), scores[:, near - tile:], FAR)
            scores = jnp.concatenate([scores[:, :near - tile], edge], 1)
            largest = jnp.max(scores, axis=1, keepdims=True)
            weights = jnp.exp2((scores - largest) * EXP2_SCALE).astype(jnp.bfloat16)
            mixed = jnp.dot(weights, value_ext, preferred_element_type=jnp.float32)
            rows = slice(part * block, (part + 1) * block)
            peak[t, rows, :] = jnp.broadcast_to(largest, (block, HD))
            total[t, rows, :] = mixed

    def attend_far(g, t):
        key_ext, value_ext = window_of(g, t * tile, far)
        for part in range(parts):
            scores = lax.dot_general(
                queries(g, t, part), key_ext, (((1,), (1,)), ((), ())),
                preferred_element_type=jnp.float32,
            )
            rows = slice(part * block, (part + 1) * block)
            before = peak[t, rows, :]
            largest = jnp.maximum(jnp.max(scores, axis=1, keepdims=True), before)
            fade = jnp.exp2((before - largest) * EXP2_SCALE)
            weights = jnp.exp2(
                (scores - jnp.concatenate([largest] * (far // HD), 1)) * EXP2_SCALE
            ).astype(jnp.bfloat16)
            mixed = jnp.dot(weights, value_ext, preferred_element_type=jnp.float32)
            mixed = total[t, rows, :] * jnp.concatenate([fade, fade], 1) + mixed
            result = (mixed[:, :HD] / mixed[:, HD:]).astype(jnp.bfloat16)
            for m in range(PAIR):
                column = (part * PAIR + m) * HD
                obuf[g, t, :, column:column + HD] = result[m * tile:(m + 1) * tile]

    for g in range(groups):
        def near_step(i, _):
            attend_near(g, (h + n_head - 1 - i) % n_head)
            if g + 1 < groups:
                @pl.when(i == 0)
                def _():
                    relay_one(0, g + 1, 0)

                @pl.when(i == 1)
                def _():
                    relay_one(0, g + 1, 1)
                    relay_two(0, g + 1, 0)
                    relay_one(1, g + 1, 0)
                    relay_two(1, g + 1, 0)

                @pl.when(i == n_head - 1)
                def _():
                    relay_one(1, g + 1, 1)
                    relay_two(1, g + 1, 1)
                    relay_two(0, g + 1, 1)
            return 0

        lax.fori_loop(0, n_head, near_step, 0)
        for a in range(2):
            arrive(g, a)

        def far_step(i, _):
            off = n_head - 1 - i
            t = (h + off) % n_head
            attend_far(g, t)

            @pl.when(i < n_head - 1)
            def _():
                deliver(g, off, t).start()

            @pl.when(i == n_head - 1)
            def _():
                keep(g).start()
            return 0

        lax.fori_loop(0, n_head, far_step, 0)

    for g in range(groups):
        for a in range(2):
            sent(g, a)
    for g in range(groups):
        keep(g).wait()
        for off in range(1, n_head):
            deliver(g, off, (h + off) % n_head).wait_send()
            receive(g, off).wait_recv()


def per_device(n_seq, n_head, queries, key_rows, value_rows, doc_lengths):
    tokens = queries.shape[0]
    groups = key_rows.shape[1] // HD
    tile = tokens // n_head
    window = SPAN * tokens
    flops = 4 * tokens * (GROUP * groups) * window * HD
    return pl.pallas_call(
        functools.partial(kernel, n_seq, n_head),
        out_shape=jax.ShapeDtypeStruct((tile, H * HD), jnp.bfloat16),
        in_specs=[pl.BlockSpec(memory_space=pltpu.SMEM)]
        + [pl.BlockSpec(memory_space=pl.ANY)] * 3,
        out_specs=pl.BlockSpec(memory_space=pl.ANY),
        scratch_shapes=[
            pltpu.VMEM((tokens, GROUP * groups * HD), jnp.bfloat16),
            pltpu.VMEM((groups, window, HD), jnp.bfloat16),
            pltpu.VMEM((groups, window, HD), jnp.bfloat16),
            pltpu.VMEM((tokens, HD), jnp.bfloat16),
            pltpu.VMEM((window, HD), jnp.bfloat16),
            pltpu.VMEM((groups, n_head, tile, GROUP * HD), jnp.bfloat16),
            pltpu.VMEM((n_head, GROUP * tile, HD), jnp.float32),
            pltpu.VMEM((n_head, GROUP * tile, 2 * HD), jnp.float32),
            pltpu.SemaphoreType.DMA((groups + 1, 2)),
            pltpu.SemaphoreType.DMA((5, groups, 2)),
            pltpu.SemaphoreType.DMA((SPAN, groups, 2)),
            pltpu.SemaphoreType.DMA((groups, n_head - 1)),
            pltpu.SemaphoreType.DMA((groups, n_head - 1)),
            pltpu.SemaphoreType.DMA((groups,)),
        ],
        compiler_params=pltpu.CompilerParams(
            collective_id=0, has_side_effects=True, vmem_limit_bytes=60 << 20
        ),
        cost_estimate=pl.CostEstimate(flops=flops, bytes_accessed=4 << 20, transcendentals=0),
    )(doc_lengths, queries, key_rows, value_rows)


def solution(mesh):
    body = functools.partial(per_device, mesh.shape["seq"], mesh.shape["head"])
    in_specs = (P("seq", "head"), P("seq", "head"), P("seq", "head"), P())
    out_specs = P(("seq", "head"), None)
    return jax.shard_map(body, mesh=mesh, in_specs=in_specs, out_specs=out_specs, check_vma=False)
```

time: 42.5 us -> 43.4 us (1.021)
  Pallas kernels: 40.1 us -> 40.9 us
    pallas_call x1, Pallas kernels: 40.1 us -> 40.9 us  [per_device(): pl.pallas_call(functools.partial(kernel, n_seq, n_head), out_shape=jax.Sh...]
where the time goes in v2:
time: 43.4 us; the launch traced here: 43.2 us
  Pallas kernels  40.9 us (94%)
  local copies, waits for them, and re-layouts  2.29 us (5%)
    pallas_call x1, Pallas kernels, per_device(): pl.pallas_call(functools.partial(kernel, n_seq, n_head), out_shape=jax.Sh...  40.9 us
    unnamed x1, local copies, waits for them, and re-layouts  2.29 us

profile of v2, /device:TPU:16, one launch (start us, length us, event | category | flops | bytes accessed | tf_op | source)
XLA Modules:
  0.0 43.2 jit_solution(4240331399828511308)
XLA Ops:
  0.0 40.9 %shard_map.46 = bf16[128,4096]{1,0:T(8,128)(2,1)} custom-call(s32[8]{0:T(128)} %doc_ref.1, bf16[512,1024]{1,0:T(8,128)(2,1)} %q_hbm.1, bf16[512,256]{1,0:T(8,128)(2,1)} %k_hbm.1, bf16[512,256]{1,0:T(8,128)(2,1)} %v_hbm.1), custom_call_target="tpu_custom_call" | custom-call | flops 4294967296 | bytes 4194304 | tf_op jit(solution)/shard_map/pallas_call | solution.py:368
  40.9 2.3 %copy.6 = bf16[128,4096]{1,0:T(8,128)(2,1)} copy(bf16[128,4096]{1,0:T(8,128)(2,1)} %shard_map.46) | data formatting | bytes 2097152

commit v3 on v2

--- a/solution.py
+++ b/solution.py
@@ -170,10 +170,12 @@
             def _():
                 copy(g, a).wait_send()
 
-    for g in range(groups):
-        for a in range(2):
-            loads[g * 2 + a].wait()
-            send_own(g, a)
+    for load in loads:
+        load.wait()
+    for a in range(2):
+        send_own(0, a)
+    for g in range(1, groups):
+        send_own(g, 0)
 
     lane = lax.broadcasted_iota(jnp.int32, (1, HD), 1)
     low = jnp.full((1, HD), 1 << 30, jnp.int32)
@@ -218,6 +220,8 @@
         relay_two(1, 0, a)
     for a in range(2):
         relay_two(0, 0, a)
+    for g in range(1, groups):
+        send_own(g, 1)
 
     near = tokens * (SPAN - 2) + tile
     far = tokens
@@ -272,11 +276,14 @@
 
     def attend_near(g, t):
         key_ext, value_ext = window_of(g, t * tile + far, near)
-        for part in range(parts):
-            scores = lax.dot_general(
+        every = [
+            lax.dot_general(
                 queries(g, t, part), key_ext, (((1,), (1,)), ((), ())),
                 preferred_element_type=jnp.float32,
             )
+            for part in range(parts)
+        ]
+        for part, scores in enumerate(every):
             edge = jnp.where(jnp.concatenate([below] * PAIR, 0), scores[:, near - tile:], FAR)
             scores = jnp.concatenate([scores[:, :near - tile], edge], 1)
             largest = jnp.max(scores, axis=1, keepdims=True)
@@ -288,11 +295,14 @@
 
     def attend_far(g, t):
         key_ext, value_ext = window_of(g, t * tile, far)
-        for part in range(parts):
-            scores = lax.dot_general(
+        every = [
+            lax.dot_general(
                 queries(g, t, part), key_ext, (((1,), (1,)), ((), ())),
                 preferred_element_type=jnp.float32,
             )
+            for part in range(parts)
+        ]
+        for part, scores in enumerate(every):
             rows = slice(part * block, (part + 1) * block)
             before = peak[t, rows, :]
             largest = jnp.maximum(jnp.max(scores, axis=1, keepdims=True), before)
@@ -311,22 +321,15 @@
         def near_step(i, _):
             attend_near(g, (h + n_head - 1 - i) % n_head)
             if g + 1 < groups:
-                @pl.when(i == 0)
+                @pl.when(i == 1)
                 def _():
                     relay_one(0, g + 1, 0)
-
-                @pl.when(i == 1)
-                def _():
-                    relay_one(0, g + 1, 1)
-                    relay_two(0, g + 1, 0)
                     relay_one(1, g + 1, 0)
                     relay_two(1, g + 1, 0)
 
                 @pl.when(i == n_head - 1)
                 def _():
-                    relay_one(1, g + 1, 1)
-                    relay_two(1, g + 1, 1)
-                    relay_two(0, g + 1, 1)
+                    relay_two(0, g + 1, 0)
             return 0
 
         lax.fori_loop(0, n_head, near_step, 0)
@@ -345,6 +348,17 @@
             @pl.when(i == n_head - 1)
             def _():
                 keep(g).start()
+
+            if g + 1 < groups:
+                @pl.when(i == n_head // 2)
+                def _():
+                    relay_one(0, g + 1, 1)
+                    relay_one(1, g + 1, 1)
+                    relay_two(1, g + 1, 1)
+
+                @pl.when(i == n_head - 1)
+                def _():
+                    relay_two(0, g + 1, 1)
             return 0
 
         lax.fori_loop(0, n_head, far_step, 0)

time: 43.4 us -> 39.7 us (0.915)
  Pallas kernels: 40.9 us -> 37.2 us
    pallas_call x1, Pallas kernels: 40.9 us -> 37.2 us  [per_device(): pl.pallas_call(functools.partial(kernel, n_seq, n_head), out_shape=jax.Sh...]
where the time goes in v3:
time: 39.7 us; the launch traced here: 39.5 us
  Pallas kernels  37.2 us (94%)
  local copies, waits for them, and re-layouts  2.29 us (6%)
    pallas_call x1, Pallas kernels, per_device(): pl.pallas_call(functools.partial(kernel, n_seq, n_head), out_shape=jax.Sh...  37.2 us
    unnamed x1, local copies, waits for them, and re-layouts  2.29 us

profile of v3, /device:TPU:16, one launch (start us, length us, event | category | flops | bytes accessed | tf_op | source)
XLA Modules:
  0.0 39.5 jit_solution(13503121676276338978)
XLA Ops:
  0.0 37.2 %shard_map.46 = bf16[128,4096]{1,0:T(8,128)(2,1)} custom-call(s32[8]{0:T(128)} %doc_ref.1, bf16[512,1024]{1,0:T(8,128)(2,1)} %q_hbm.1, bf16[512,256]{1,0:T(8,128)(2,1)} %k_hbm.1, bf16[512,256]{1,0:T(8,128)(2,1)} %v_hbm.1), custom_call_target="tpu_custom_call" | custom-call | flops 4294967296 | bytes 4194304 | tf_op jit(solution)/shard_map/pallas_call | solution.py:382
  37.3 2.3 %copy.6 = bf16[128,4096]{1,0:T(8,128)(2,1)} copy(bf16[128,4096]{1,0:T(8,128)(2,1)} %shard_map.46) | data formatting | bytes 2097152

commit v4 on v3

--- a/solution.py
+++ b/solution.py
@@ -73,7 +73,7 @@
     pl.semaphore_wait(barrier, n_head + beyond)
 
     own = SPAN - 1
-    cut = tokens // 48 * 16
+    cut = tokens // 64 * 16
 
     def hop(kind, g, a, source, target, slot, piece=None):
         start, size = {None: (0, tokens), 0: (0, cut), 1: (cut, tokens - cut)}[piece]
@@ -271,8 +271,12 @@
     def window_of(g, start, size):
         keys = pl.ds(pl.multiple_of(start, tile), size)
         key_ext = jnp.concatenate([kbuf[g, keys, :], kdoc[keys, :]], 1)
-        value_ext = jnp.concatenate([vbuf[g, keys, :], jnp.ones((size, HD), jnp.bfloat16)], 1)
-        return key_ext, value_ext
+        return key_ext, vbuf[g, keys, :]
+
+    def mix(weights, values):
+        mixed = jnp.dot(weights.astype(jnp.bfloat16), values, preferred_element_type=jnp.float32)
+        amount = jnp.sum(weights, axis=1, keepdims=True)
+        return jnp.concatenate([mixed, jnp.broadcast_to(amount, (block, HD))], 1)
 
     def attend_near(g, t):
         key_ext, value_ext = window_of(g, t * tile + far, near)
@@ -287,8 +291,8 @@
             edge = jnp.where(jnp.concatenate([below] * PAIR, 0), scores[:, near - tile:], FAR)
             scores = jnp.concatenate([scores[:, :near - tile], edge], 1)
             largest = jnp.max(scores, axis=1, keepdims=True)
-            weights = jnp.exp2((scores - largest) * EXP2_SCALE).astype(jnp.bfloat16)
-            mixed = jnp.dot(weights, value_ext, preferred_element_type=jnp.float32)
+            weights = jnp.exp2((scores - largest) * EXP2_SCALE)
+            mixed = mix(weights, value_ext)
             rows = slice(part * block, (part + 1) * block)
             peak[t, rows, :] = jnp.broadcast_to(largest, (block, HD))
             total[t, rows, :] = mixed
@@ -309,8 +313,8 @@
             fade = jnp.exp2((before - largest) * EXP2_SCALE)
             weights = jnp.exp2(
                 (scores - jnp.concatenate([largest] * (far // HD), 1)) * EXP2_SCALE
-            ).astype(jnp.bfloat16)
-            mixed = jnp.dot(weights, value_ext, preferred_element_type=jnp.float32)
+            )
+            mixed = mix(weights, value_ext)
             mixed = total[t, rows, :] * jnp.concatenate([fade, fade], 1) + mixed
             result = (mixed[:, :HD] / mixed[:, HD:]).astype(jnp.bfloat16)
             for m in range(PAIR):

time: 39.7 us -> 38.7 us (0.975)
  Pallas kernels: 37.2 us -> 36.3 us
    pallas_call x1, Pallas kernels: 37.2 us -> 36.3 us  [per_device(): pl.pallas_call(functools.partial(kernel, n_seq, n_head), out_shape=jax.Sh...]
where the time goes in v4:
time: 38.7 us; the launch traced here: 38.6 us
  Pallas kernels  36.3 us (94%)
  local copies, waits for them, and re-layouts  2.29 us (6%)
    pallas_call x1, Pallas kernels, per_device(): pl.pallas_call(functools.partial(kernel, n_seq, n_head), out_shape=jax.Sh...  36.3 us
    unnamed x1, local copies, waits for them, and re-layouts  2.29 us

profile of v4, /device:TPU:16, one launch (start us, length us, event | category | flops | bytes accessed | tf_op | source)
XLA Modules:
  0.0 38.6 jit_solution(542049069475777763)
XLA Ops:
  0.0 36.3 %shard_map.46 = bf16[128,4096]{1,0:T(8,128)(2,1)} custom-call(s32[8]{0:T(128)} %doc_ref.1, bf16[512,1024]{1,0:T(8,128)(2,1)} %q_hbm.1, bf16[512,256]{1,0:T(8,128)(2,1)} %k_hbm.1, bf16[512,256]{1,0:T(8,128)(2,1)} %v_hbm.1), custom_call_target="tpu_custom_call" | custom-call | flops 4294967296 | bytes 4194304 | tf_op jit(solution)/shard_map/pallas_call | solution.py:386
  36.3 2.3 %copy.6 = bf16[128,4096]{1,0:T(8,128)(2,1)} copy(bf16[128,4096]{1,0:T(8,128)(2,1)} %shard_map.46) | data formatting | bytes 2097152
